TPU v7x, 32 devices: a whole 2x2x4 slice. The times are simulated.
32 devices in a mesh: role: 2 (over y), tile: 16 (over z, x, core).
Axes of the slice: x: 2, y: 2, z: 4, core: 2. Of those that a mesh axis runs over, the one named last changes fastest.
Arguments:
- fields_pair: float32 [2, 512, 16384], P('role', None, 'tile'), may hold values from 0 to 1
- velocity: float32 [16384], P('tile'), may hold values from -0.5 to 0.5
- growth: float32 [16384], P('tile'), may hold values from 0.05 to 0.5
- features: bfloat16 [512, 1024], replicated, may hold values from -6 to 6
- assignment: int32 [512], replicated, may hold values from 0 to 511, each once
- out_pair: float32 [2, 1024, 16384], P('role', None, 'tile'), may hold values from -0.1875 to 0.1875
- hidden_pair: float32 [2, 5, 1024, 1024], P('role', None, 'tile'), may hold values from -0.1875 to 0.1875
Outputs:
- fields_next: float32 [2, 512, 16384], P('role', None, 'tile')
- out_next: float32 [2, 1024, 16384], P('role', None, 'tile')
- hidden_next: float32 [2, 5, 1024, 1024], P('role', None, 'tile')
Inputs may be any that keep to these rules, and one draw needn't show every extreme that they name: `assignment`: a permutation of the 512 members.
All inputs are finite; a program needn't handle non-finite values.
Results may differ from a plain program's by a relative error of at most 0.0022.
The roundings to bfloat16 on the way count: a program that leaves them out, or rounds other values in their place, can miss the bound.
Values may be sent and summed in bfloat16 or wider, within the bound.
A program may use at most 192 MiB of HBM per device.

v0:
```python
import jax
import jax.numpy as jnp
from jax import lax
from jax.sharding import PartitionSpec as P

momentum_decay = 0.9
step_size = 0.1


def extended(value, axis, dim, width):
    count, length = (lax.axis_size(axis), value.shape[dim])
    up = [(i, (i + 1) % count) for i in range(count)]
    down = [(j, i) for i, j in up]
    last = lax.slice_in_dim(value, length - width, length, axis=dim)
    leading = lax.slice_in_dim(value, 0, width, axis=dim)
    before = lax.ppermute(last, axis, up)
    after = lax.ppermute(leading, axis, down)
    return jnp.concatenate([before, value, after], axis=dim)


def silu_slope(values):
    logistic = jax.nn.sigmoid(values)
    return logistic * (1.0 + values * (1.0 - logistic))


def advance(padded, growth):
    states = padded[:-1]
    velocity_row = padded[-1]
    outflow = (
        jnp.maximum(velocity_row[:-1], 0.0) * states[:, :-1]
        + jnp.minimum(velocity_row[:-1], 0.0) * states[:, 1:]
    )
    carried = states[:, 1:-1] - outflow[:, 1:] + outflow[:, :-1]
    return carried + growth * carried * (1.0 - carried)


def to_trainer(value):
    return lax.ppermute(value.astype(jnp.bfloat16), "role", [(0, 1)])


def to_solver(value):
    return lax.ppermute(value.astype(jnp.bfloat16), "role", [(1, 0)])


def plain_training(features, hidden_narrow, out_narrow, own_fields, own_out, own_hidden):
    layer_count, unit_rows = own_hidden.shape[:2]
    batch = own_fields.shape[0]
    first_unit = lax.axis_index("tile") * unit_rows
    momentum_out = to_trainer(own_out)
    momentum_hidden = to_trainer(own_hidden)
    full_hidden = [
        lax.all_gather(hidden_narrow[i], "tile", axis=0, tiled=True) for i in range(layer_count)
    ]
    inputs, summed_list = ([], [])
    activation = features
    for i in range(layer_count):
        inputs.append(activation)
        summed = jnp.dot(activation, full_hidden[i], preferred_element_type=jnp.float32)
        summed_list.append(summed)
        activation = jax.nn.silu(summed).astype(jnp.bfloat16)
    predicted = jnp.dot(activation, out_narrow, preferred_element_type=jnp.float32)
    residual = ((predicted - own_fields) / batch).astype(jnp.bfloat16)
    partial_grad = lax.dot_general(
        residual, out_narrow, (((1,), (1,)), ((), ())), preferred_element_type=jnp.float32
    )
    upstream = lax.psum(partial_grad, "tile")
    grad_out = jnp.dot(activation.T, residual, preferred_element_type=jnp.float32)
    sent_out = to_solver(grad_out)
    gradients, sent = ([], [])
    for i in reversed(range(layer_count)):
        slope = (upstream * silu_slope(summed_list[i])).astype(jnp.bfloat16)
        own_inputs = lax.dynamic_slice_in_dim(inputs[i], first_unit, unit_rows, 1)
        gradient = jnp.dot(own_inputs.T, slope, preferred_element_type=jnp.float32)
        gradients.append(gradient)
        sent.append(to_solver(gradient))
        if i > 0:
            upstream = lax.dot_general(
                slope, full_hidden[i], (((1,), (1,)), ((), ())), preferred_element_type=jnp.float32
            )
    solver_side = lax.axis_index("role") == 0
    other_out = jnp.where(solver_side, sent_out, momentum_out)
    other_hidden = jnp.where(solver_side, jnp.stack(sent[::-1]), momentum_hidden)
    return (grad_out, jnp.stack(gradients[::-1]), other_out, other_hidden)


def body(fields_pair, velocity, growth, features, assignment, out_pair, hidden_pair):
    solver_side = lax.axis_index("role") == 0
    own_fields = fields_pair[0]
    own_out = out_pair[0]
    own_hidden = hidden_pair[0]
    stacked = jnp.concatenate([own_fields, velocity[None, :]], axis=0)
    advanced = advance(extended(stacked, "tile", 1, 1), growth)
    fresh_fields = to_trainer(advanced)
    grad_out, grad_hidden, other_out, other_hidden = plain_training(
        features,
        own_hidden.astype(jnp.bfloat16),
        own_out.astype(jnp.bfloat16),
        own_fields,
        own_out,
        own_hidden,
    )
    grad_out, grad_hidden, other_out, other_hidden = (
        v.astype(jnp.float32) for v in (grad_out, grad_hidden, other_out, other_hidden)
    )
    out_next = jnp.where(
        solver_side,
        momentum_decay * own_out + other_out,
        own_out - step_size * (momentum_decay * other_out + grad_out),
    )
    hidden_next = jnp.where(
        solver_side,
        momentum_decay * own_hidden + other_hidden,
        own_hidden - step_size * (momentum_decay * other_hidden + grad_hidden),
    )
    next_batch = jnp.take(fresh_fields, assignment, axis=0).astype(jnp.float32)
    fields_next = jnp.where(solver_side, advanced, next_batch)
    return (fields_next[None], out_next[None], hidden_next[None])


def solution(mesh):
    return jax.shard_map(
        body,
        mesh=mesh,
        in_specs=(
            P("role", None, "tile"),
            P("tile"),
            P("tile"),
            P(),
            P(),
            P("role", None, "tile"),
            P("role", None, "tile", None),
        ),
        out_specs=(P("role", None, "tile"), P("role", None, "tile"), P("role", None, "tile", None)),
        check_vma=False,
    )
```

profile of v0, /device:TPU:0, one launch (start us, length us, event | category | flops | bytes accessed | tf_op | source)
XLA Modules:
  0.0 390.6 jit_solution(13564146009136946338)
XLA Ops:
  7.2 0.0 all-gather.11.cloned.1.call-start
  7.2 1.5 bitcast_convert_fusion.1
  8.7 0.8 copy-done.6
  9.5 0.8 fusion.60
  10.4 0.0 all-gather.13.cloned.1.call-start
  10.5 0.7 all-gather.13.cloned.1.call-update
  11.2 0.0 all-gather.15.cloned.1.call-start
  11.2 0.7 all-gather.15.cloned.1.call-update
  11.9 0.0 all-gather.17.cloned.1.call-start
  11.9 0.5 all-gather.17.cloned.1.call-update
  12.5 0.0 all-gather.19.cloned.1.call-start
  12.5 0.5 all-gather.19.cloned.1.call-update
  13.1 5.9 %collective-permute-start.10 = (bf16[5,64,1024]{2,1,0:T(8,128)(2,1)}, bf16[5,64,1024]{2,1,0:T(8,128)(2,1)}, u32[]{:S(2)}, u32[]{:S(2)}) collective-permute-start(bf16[5,64,1024]{2,1,0:T(8,128)(2,1)} %copy-done.6), channel_id=1, source_target_pairs={{0,16},{1,17},{2,18},{3,19},{4,20},{5,21},{6,22},{7,23},{8,24},{9,... | collective-permute-start | bytes 1966088 | tf_op jit(solution)/shard_map/ppermute | solution.py:38
  19.0 4.0 %bitcast_convert_fusion = bf16[1024,1024]{1,0:T(8,128)(2,1)} fusion(f32[1,1024,1024]{2,1,0:T(8,128)} %param.12), kind=kLoop, calls=%fused_computation.8 | loop fusion | flops 1048576 | bytes 6291456 | tf_op jit(solution)/shard_map/convert_element_type | solution.py:97
  23.0 2.8 collective-permute-start.4
  25.8 0.1 pad_maximum_fusion.5
  25.9 0.1 collective-permute-start
  26.0 4.4 %collective-permute-start.1 = (f32[513,1]{1,0:T(8,128)S(1)}, f32[513,1]{1,0:T(8,128)S(1)}, u32[]{:S(2)}, u32[]{:S(2)}) collective-permute-start(f32[513,1]{1,0:T(8,128)S(1)} %get-tuple-element.8), channel_id=1, source_target_pairs={{1,0},{2,1},{3,2},{4,3},{5,4},{6,5},{7,6},{8,7},{9,8},{10,9},{11,1... | collective-permute-start | bytes 6164 | tf_op jit(solution)/shard_map/ppermute | solution.py:17
  30.4 5.4 %collective-permute-done = f32[513,1]{1,0:T(8,128)S(1)} collective-permute-done((f32[513,1]{1,0:T(8,128)S(1)}, f32[513,1]{1,0:T(8,128)S(1)}, u32[]{:S(2)}, u32[]{:S(2)}) %collective-permute-start) | collective-permute-done | bytes 2084 | tf_op jit(solution)/shard_map/ppermute | solution.py:16
  35.8 0.1 maximum_reduce_fusion
  36.0 0.7 fusion.6
  36.7 2.4 fusion.59
  39.1 1.5 collective-permute-start.2
  40.6 15.2 %all-gather.11.cloned.1.call-done = bf16[1,1024,1024]{2,1,0:T(8,128)(2,1)} async-done(((bf16[1,64,1024]{2,1,0:T(8,128)(2,1)}), bf16[1,1024,1024]{2,1,0:T(8,128)(2,1)}) %all-gather.11.cloned.1.call-update) | async-done | bytes 2097168 | tf_op jit(solution)/shard_map/all_gather | solution.py:52
  55.8 4.6 %multiply_convert_fusion.10 = (bf16[512,1024]{1,0:T(8,128)(2,1)}, f32[512,1024]{1,0:T(8,128)}) fusion(bf16[512,1024]{1,0:T(8,128)(2,1)S(1)} %copy-done, bf16[1,1024,1024]{2,1,0:T(8,128)(2,1)} %all-gather.11.cloned.1.call-done), kind=kOutput, calls=%fused_computation.51 | convolution fusion | flops 1076363264 | bytes 6291456 | tf_op jit(solution)/shard_map/dot_general | solution.py:58
  60.5 37.8 %all-gather.13.cloned.1.call-done = bf16[1,1024,1024]{2,1,0:T(8,128)(2,1)} async-done(((bf16[1,64,1024]{2,1,0:T(8,128)(2,1)}), bf16[1,1024,1024]{2,1,0:T(8,128)(2,1)}) %all-gather.13.cloned.1.call-update) | async-done | bytes 2097168 | tf_op jit(solution)/shard_map/all_gather | solution.py:52
  98.2 4.7 %multiply_convert_fusion.9 = (bf16[512,1024]{1,0:T(8,128)(2,1)S(1)}, f32[512,1024]{1,0:T(8,128)}) fusion(bf16[512,1024]{1,0:T(8,128)(2,1)} %get-tuple-element.14, bf16[1,1024,1024]{2,1,0:T(8,128)(2,1)} %all-gather.13.cloned.1.call-done), kind=kOutput, calls=%fused_computation.49 | convolution fusion | flops 1076363264 | bytes 6291456 | tf_op jit(solution)/shard_map/dot_general | solution.py:58
  102.9 37.7 %all-gather.15.cloned.1.call-done = bf16[1,1024,1024]{2,1,0:T(8,128)(2,1)} async-done(((bf16[1,64,1024]{2,1,0:T(8,128)(2,1)}), bf16[1,1024,1024]{2,1,0:T(8,128)(2,1)}) %all-gather.15.cloned.1.call-update) | async-done | bytes 2097168 | tf_op jit(solution)/shard_map/all_gather | solution.py:52
  140.6 4.7 %multiply_convert_fusion.8 = (bf16[512,1024]{1,0:T(8,128)(2,1)}, f32[512,1024]{1,0:T(8,128)}) fusion(bf16[512,1024]{1,0:T(8,128)(2,1)S(1)} %get-tuple-element.16, bf16[1,1024,1024]{2,1,0:T(8,128)(2,1)} %all-gather.15.cloned.1.call-done), kind=kOutput, calls=%fused_computation.47 | convolution fusion | flops 1076363264 | bytes 6291456 | tf_op jit(solution)/shard_map/dot_general | solution.py:58
  145.3 37.5 %all-gather.17.cloned.1.call-done = bf16[1,1024,1024]{2,1,0:T(8,128)(2,1)} async-done(((bf16[1,64,1024]{2,1,0:T(8,128)(2,1)}), bf16[1,1024,1024]{2,1,0:T(8,128)(2,1)}) %all-gather.17.cloned.1.call-update) | async-done | bytes 2097168 | tf_op jit(solution)/shard_map/all_gather | solution.py:52
  182.8 4.7 %multiply_convert_fusion.7 = (bf16[512,1024]{1,0:T(8,128)(2,1)S(1)}, f32[512,1024]{1,0:T(8,128)}) fusion(bf16[512,1024]{1,0:T(8,128)(2,1)} %get-tuple-element.18, bf16[1,1024,1024]{2,1,0:T(8,128)(2,1)} %all-gather.17.cloned.1.call-done), kind=kOutput, calls=%fused_computation.45 | convolution fusion | flops 1076363264 | bytes 6291456 | tf_op jit(solution)/shard_map/dot_general | solution.py:58
  187.6 38.1 %all-gather.19.cloned.1.call-done = bf16[1,1024,1024]{2,1,0:T(8,128)(2,1)} async-done(((bf16[1,64,1024]{2,1,0:T(8,128)(2,1)}), bf16[1,1024,1024]{2,1,0:T(8,128)(2,1)}) %all-gather.19.cloned.1.call-update) | async-done | bytes 2097168 | tf_op jit(solution)/shard_map/all_gather | solution.py:52
  225.6 3.0 fusion.10
  228.7 3.7 multiply_convert_fusion.5
  232.3 1.0 copy-done.19
  233.3 4.2 %fusion.64 = f32[512,1024]{1,0:T(8,128)} fusion(bf16[512,1024]{1,0:T(8,128)(2,1)S(1)} %multiply_convert_fusion.5, bf16[1024,1024]{1,0:T(8,128)(2,1)} %bitcast_convert_fusion), kind=kOutput, calls=%fused_computation.103 | convolution fusion | flops 1073741824 | bytes 5242880 | tf_op jit(solution)/shard_map/dot_general | solution.py:63
  237.6 2.1 gather_fusion
  239.6 3.4 select_bitcast_fusion
  243.0 4.1 %fusion.61 = (bf16[1024,1024]{1,0:T(8,128)(2,1)}, f32[1024,1024]{1,0:T(8,128)}) fusion(bf16[512,1024]{1,0:T(8,128)(2,1)S(1)} %copy-done.20, f32[512,1024]{1,0:T(8,128)S(1)} %copy-done.8), kind=kOutput, calls=%fused_computation.102 | convolution fusion | flops 1077411840 | bytes 9437184 | tf_op jit(solution)/shard_map/dot_general | solution.py:67
  247.1 1.5 collective-permute-start.3
  248.6 86.0 %all-reduce.2.cloned.1.call-done = f32[512,1024]{1,0:T(8,128)} async-done(((f32[512,1024]{1,0:T(8,128)}), f32[512,1024]{1,0:T(8,128)}) %all-reduce.2.cloned.1.call-update) | async-done | bytes 2097168 | tf_op jit(solution)/shard_map/psum | solution.py:66
  334.6 3.0 multiply_convert_fusion.4
  337.5 4.0 %multiply_convert_fusion.3 = bf16[512,1024]{1,0:T(8,128)(2,1)S(1)} fusion(f32[512,1024]{1,0:T(8,128)} %get-tuple-element.21, bf16[512,1024]{1,0:T(8,128)(2,1)S(1)} %multiply_convert_fusion.4, bf16[1,1024,1024]{2,1,0:T(8,128)(2,1)} %all-gather.19.cloned.1.call-done), kind=kOutput, calls=%fused_computation.40 | convolution fusion | flops 1078460416 | bytes 6291456 | tf_op jit(solution)/shard_map/dot_general | solution.py:77
  341.6 1.6 multiply_convert_fusion.2
  343.2 0.3 copy-done.17
  343.5 0.6 copy-done.21
  344.1 2.6 multiply_convert_fusion.1
  346.7 4.3 %bitcast_dynamic-update-slice_fusion.4 = (f32[5,64,1024]{2,1,0:T(8,128)S(1)}, bf16[64,1024]{1,0:T(8,128)(2,1)S(1)}) fusion(f32[512,1024]{1,0:T(8,128)} %get-tuple-element.15, bf16[512,1024]{1,0:T(8,128)(2,1)} %multiply_convert_fusion.1, bf16[1,1024,1024]{2,1,0:T(8,128)(2,1)} %all-gather.13.cloned.1.call-done, bf16[512,1024]{1,0:T(8,128)(2,1)S(1)} %copy-done, ...), kind=kOutput, calls=%fused_computation.72 | convolution fusion | flops 1145634816 | bytes 5767172 | tf_op jit(solution)/shard_map/dot_general | solution.py:73
  351.1 1.8 bitcast_dynamic-update-slice_fusion.3
  352.9 1.3 collective-permute-start.6
  354.2 1.3 collective-permute-start.5
  355.5 1.7 bitcast_dynamic-update-slice_fusion.2
  357.2 1.5 bitcast_dynamic-update-slice_fusion.1
  358.7 1.5 bitcast_dynamic-update-slice_fusion
  360.2 1.8 collective-permute-done.5
  362.0 1.3 collective-permute-start.7
  363.3 1.3 collective-permute-start.8
  364.6 4.2 %collective-permute-done.7 = bf16[64,1024]{1,0:T(8,128)(2,1)S(1)} collective-permute-done((bf16[64,1024]{1,0:T(8,128)(2,1)S(1)}, bf16[64,1024]{1,0:T(8,128)(2,1)S(1)}, u32[]{:S(2)}, u32[]{:S(2)}) %collective-permute-start.7) | collective-permute-done | bytes 131104 | tf_op jit(solution)/shard_map/ppermute | solution.py:42
  368.8 1.3 collective-permute-start.9
  370.1 0.1 collective-permute-done.8
  370.2 5.4 %collective-permute-done.9 = bf16[64,1024]{1,0:T(8,128)(2,1)S(1)} collective-permute-done((bf16[64,1024]{1,0:T(8,128)(2,1)S(1)}, bf16[64,1024]{1,0:T(8,128)(2,1)S(1)}, u32[]{:S(2)}, u32[]{:S(2)}) %collective-permute-start.9) | collective-permute-done | bytes 131104 | tf_op jit(solution)/shard_map/ppermute | solution.py:42
  375.7 1.6 fusion.35
  377.3 1.1 copy-done.3
  378.4 5.3 %fusion.1 = f32[1,1024,1024]{2,1,0:T(8,128)} fusion(f32[1024,1024]{1,0:T(8,128)S(1)} %copy-done.5, f32[1,1024,1024]{2,1,0:T(8,128)S(1)} %copy-done.3, bf16[1024,1024]{1,0:T(8,128)(2,1)} %collective-permute-done.3, bf16[1024,1024]{1,0:T(8,128)(2,1)} %collective-permute-done.4, pred[]{:T(512)S(6)} %eq.4), kind=kLoop, calls=%fused_computation.4 | loop fusion | flops 9437184 | bytes 16777216 | tf_op jit(solution)/shard_map/broadcast_in_dim | solution.py:117
  (58 shorter events, 0.3 us)
Async XLA Ops:
  7.2 48.7 %copy-start = (bf16[512,1024]{1,0:T(8,128)(2,1)S(1)}, bf16[512,1024]{1,0:T(8,128)(2,1)}, u32[]{:S(2)}) copy-start(bf16[512,1024]{1,0:T(8,128)(2,1)} %param.10) | copy-start | bytes 3145732
  7.2 48.7 %all-gather.11.cloned.1.call-start = ((), (), s32[]{:S(2)}) async-start(), calls=%async_computation.1 | async-start | bytes 2228224 | tf_op jit(solution)/shard_map/all_gather | solution.py:52
  8.7 0.8 copy-start.6
  10.4 87.8 %all-gather.13.cloned.1.call-start = ((), (), s32[]{:S(2)}) async-start(), calls=%async_computation.2 | async-start | bytes 2228224 | tf_op jit(solution)/shard_map/all_gather | solution.py:52
  11.2 129.5 %all-gather.15.cloned.1.call-start = ((), (), s32[]{:S(2)}) async-start(), calls=%async_computation.3 | async-start | bytes 2228224 | tf_op jit(solution)/shard_map/all_gather | solution.py:52
  11.9 170.9 %all-gather.17.cloned.1.call-start = ((), (), s32[]{:S(2)}) async-start(), calls=%async_computation.4 | async-start | bytes 2228224 | tf_op jit(solution)/shard_map/all_gather | solution.py:52
  12.5 213.2 %all-gather.19.cloned.1.call-start = ((), (), s32[]{:S(2)}) async-start(), calls=%async_computation.5 | async-start | bytes 2228224 | tf_op jit(solution)/shard_map/all_gather | solution.py:52
  13.1 12.7 %copy-start.1 = (f32[1,512,1024]{2,1,0:T(8,128)S(1)}, f32[1,512,1024]{2,1,0:T(8,128)}, u32[]{:S(2)}) copy-start(f32[1,512,1024]{2,1,0:T(8,128)} %param.7) | copy-start | bytes 6291460
  13.1 12.7 %copy-start.12 = (f32[1024]{0:T(1024)S(1)}, f32[1024]{0:T(1024)}, u32[]{:S(2)}) copy-start(f32[1024]{0:T(1024)} %param.8) | copy-start | bytes 12292
  13.1 321.5 %all-reduce.2.cloned.1.call-start = ((), (), s32[]{:S(2)}) async-start(), calls=%async_computation | async-start | bytes 4194304 | tf_op jit(solution)/shard_map/psum | solution.py:66
  13.1 362.6 %collective-permute-start.10 = (bf16[5,64,1024]{2,1,0:T(8,128)(2,1)}, bf16[5,64,1024]{2,1,0:T(8,128)(2,1)}, u32[]{:S(2)}, u32[]{:S(2)}) collective-permute-start(bf16[5,64,1024]{2,1,0:T(8,128)(2,1)} %copy-done.6), channel_id=1, source_target_pairs={{0,16},{1,17},{2,18},{3,19},{4,20},{5,21},{6,22},{7,23},{8,24},{9,... | collective-permute-start | bytes 1966088 | tf_op jit(solution)/shard_map/ppermute | solution.py:38
  23.0 7.4 %copy-start.15 = (s32[512]{0:T(512)S(1)}, s32[512]{0:T(512)}, u32[]{:S(2)}) copy-start(s32[512]{0:T(512)} %param.11) | copy-start | bytes 6148
  23.0 354.3 %collective-permute-start.4 = (bf16[1024,1024]{1,0:T(8,128)(2,1)}, bf16[1024,1024]{1,0:T(8,128)(2,1)}, u32[]{:S(2)}, u32[]{:S(2)}) collective-permute-start(bf16[1024,1024]{1,0:T(8,128)(2,1)} %bitcast_convert_fusion), channel_id=1, source_target_pairs={{0,16},{1,17},{2,18},{3,19},{4,20},{5,21},{6,22},{7,23},{8,24},{9,... | collective-permute-start | bytes 6291464 | tf_op jit(solution)/shard_map/ppermute | solution.py:38
  25.9 9.9 %collective-permute-start = (f32[513,1]{1,0:T(8,128)S(1)}, f32[513,1]{1,0:T(8,128)S(1)}, u32[]{:S(2)}, u32[]{:S(2)}) collective-permute-start(f32[513,1]{1,0:T(8,128)S(1)} %get-tuple-element.7), channel_id=1, source_target_pairs={{0,1},{1,2},{2,3},{3,4},{4,5},{5,6},{6,7},{7,8},{8,9},{9,10},{10,1... | collective-permute-start | bytes 6164 | tf_op jit(solution)/shard_map/ppermute | solution.py:16
  26.0 10.0 %collective-permute-start.1 = (f32[513,1]{1,0:T(8,128)S(1)}, f32[513,1]{1,0:T(8,128)S(1)}, u32[]{:S(2)}, u32[]{:S(2)}) collective-permute-start(f32[513,1]{1,0:T(8,128)S(1)} %get-tuple-element.8), channel_id=1, source_target_pairs={{1,0},{2,1},{3,2},{4,3},{5,4},{6,5},{7,6},{8,7},{9,8},{10,9},{11,1... | collective-permute-start | bytes 6164 | tf_op jit(solution)/shard_map/ppermute | solution.py:17
  35.9 0.7 copy-start.16
  39.1 198.5 %collective-permute-start.2 = (bf16[512,1024]{1,0:T(8,128)(2,1)}, bf16[512,1024]{1,0:T(8,128)(2,1)S(1)}, u32[]{:S(2)}, u32[]{:S(2)}) collective-permute-start(bf16[512,1024]{1,0:T(8,128)(2,1)} %get-tuple-element.5), channel_id=1, source_target_pairs={{0,16},{1,17},{2,18},{3,19},{4,20},{5,21},{6,22},{7,23},{8,24},{9,... | collective-permute-start | bytes 3145736 | tf_op jit(solution)/shard_map/ppermute | solution.py:38
  102.9 42.4 %copy-start.13 = (bf16[512,1024]{1,0:T(8,128)(2,1)}, bf16[512,1024]{1,0:T(8,128)(2,1)S(1)}, u32[]{:S(2)}) copy-start(bf16[512,1024]{1,0:T(8,128)(2,1)S(1)} %get-tuple-element.16) | copy-start | bytes 3145732
  187.5 41.1 %copy-start.14 = (bf16[512,1024]{1,0:T(8,128)(2,1)}, bf16[512,1024]{1,0:T(8,128)(2,1)S(1)}, u32[]{:S(2)}) copy-start(bf16[512,1024]{1,0:T(8,128)(2,1)S(1)} %get-tuple-element.20) | copy-start | bytes 3145732
  225.6 3.0 copy-start.2
  228.6 3.7 copy-start.7
  232.3 1.0 copy-start.19
  239.6 3.4 copy-start.8
  239.6 3.4 copy-start.20
  247.1 130.3 %collective-permute-start.3 = (bf16[1024,1024]{1,0:T(8,128)(2,1)}, bf16[1024,1024]{1,0:T(8,128)(2,1)}, u32[]{:S(2)}, u32[]{:S(2)}) collective-permute-start(bf16[1024,1024]{1,0:T(8,128)(2,1)} %get-tuple-element.22), channel_id=1, source_target_pairs={{16,0},{17,1},{18,2},{19,3},{20,4},{21,5},{22,6},{23,7},{24,8},{25... | collective-permute-start | bytes 6291464 | tf_op jit(solution)/shard_map/ppermute | solution.py:42
  337.5 4.0 %copy-start.18 = (bf16[1,1024,1024]{2,1,0:T(8,128)(2,1)S(1)}, bf16[1,1024,1024]{2,1,0:T(8,128)(2,1)}, u32[]{:S(2)}) copy-start(bf16[1,1024,1024]{2,1,0:T(8,128)(2,1)} %all-gather.17.cloned.1.call-done) | copy-start | bytes 6291460
  337.5 4.0 %copy-start.22 = (f32[512,1024]{1,0:T(8,128)S(1)}, f32[512,1024]{1,0:T(8,128)}, u32[]{:S(2)}) copy-start(f32[512,1024]{1,0:T(8,128)} %get-tuple-element.19) | copy-start | bytes 6291460
  341.5 1.7 copy-start.9
  341.5 2.0 copy-start.17
  341.5 2.6 copy-start.21
  343.2 3.5 copy-start.11
  351.1 6.1 %copy-start.10 = (bf16[512,1024]{1,0:T(8,128)(2,1)S(1)}, bf16[512,1024]{1,0:T(8,128)(2,1)}, u32[]{:S(2)}) copy-start(bf16[512,1024]{1,0:T(8,128)(2,1)} %copy-done.9) | copy-start | bytes 3145732
  352.9 10.4 %collective-permute-start.6 = (bf16[64,1024]{1,0:T(8,128)(2,1)S(1)}, bf16[64,1024]{1,0:T(8,128)(2,1)S(1)}, u32[]{:S(2)}, u32[]{:S(2)}) collective-permute-start(bf16[64,1024]{1,0:T(8,128)(2,1)S(1)} %get-tuple-element.27), channel_id=1, source_target_pairs={{16,0},{17,1},{18,2},{19,3},{20,4},{21,5},{22,6},{23,7},{24,8},{25... | collective-permute-start | bytes 393224 | tf_op jit(solution)/shard_map/ppermute | solution.py:42
  354.2 7.8 %collective-permute-start.5 = (bf16[64,1024]{1,0:T(8,128)(2,1)S(1)}, bf16[64,1024]{1,0:T(8,128)(2,1)S(1)}, u32[]{:S(2)}, u32[]{:S(2)}) collective-permute-start(bf16[64,1024]{1,0:T(8,128)(2,1)S(1)} %get-tuple-element.25), channel_id=1, source_target_pairs={{16,0},{17,1},{18,2},{19,3},{20,4},{21,5},{22,6},{23,7},{24,8},{25... | collective-permute-start | bytes 393224 | tf_op jit(solution)/shard_map/ppermute | solution.py:42
  357.2 18.5 %copy-start.4 = (f32[1,5,64,1024]{3,2,1,0:T(8,128)S(1)}, f32[1,5,64,1024]{3,2,1,0:T(8,128)}, u32[]{:S(2)}) copy-start(f32[1,5,64,1024]{3,2,1,0:T(8,128)} %param.13) | copy-start | bytes 3932164
  357.2 20.1 %copy-start.5 = (f32[1024,1024]{1,0:T(8,128)S(1)}, f32[1024,1024]{1,0:T(8,128)}, u32[]{:S(2)}) copy-start(f32[1024,1024]{1,0:T(8,128)} %get-tuple-element.23) | copy-start | bytes 12582916
  362.0 6.8 %collective-permute-start.7 = (bf16[64,1024]{1,0:T(8,128)(2,1)S(1)}, bf16[64,1024]{1,0:T(8,128)(2,1)S(1)}, u32[]{:S(2)}, u32[]{:S(2)}) collective-permute-start(bf16[64,1024]{1,0:T(8,128)(2,1)S(1)} %get-tuple-element.29), channel_id=1, source_target_pairs={{16,0},{17,1},{18,2},{19,3},{20,4},{21,5},{22,6},{23,7},{24,8},{25... | collective-permute-start | bytes 393224 | tf_op jit(solution)/shard_map/ppermute | solution.py:42
  363.3 6.9 %collective-permute-start.8 = (bf16[64,1024]{1,0:T(8,128)(2,1)S(1)}, bf16[64,1024]{1,0:T(8,128)(2,1)S(1)}, u32[]{:S(2)}, u32[]{:S(2)}) collective-permute-start(bf16[64,1024]{1,0:T(8,128)(2,1)S(1)} %get-tuple-element.31), channel_id=1, source_target_pairs={{16,0},{17,1},{18,2},{19,3},{20,4},{21,5},{22,6},{23,7},{24,8},{25... | collective-permute-start | bytes 393224 | tf_op jit(solution)/shard_map/ppermute | solution.py:42
  368.8 6.8 %collective-permute-start.9 = (bf16[64,1024]{1,0:T(8,128)(2,1)S(1)}, bf16[64,1024]{1,0:T(8,128)(2,1)S(1)}, u32[]{:S(2)}, u32[]{:S(2)}) collective-permute-start(bf16[64,1024]{1,0:T(8,128)(2,1)S(1)} %get-tuple-element.33), channel_id=1, source_target_pairs={{16,0},{17,1},{18,2},{19,3},{20,4},{21,5},{22,6},{23,7},{24,8},{25... | collective-permute-start | bytes 393224 | tf_op jit(solution)/shard_map/ppermute | solution.py:42
  375.7 2.7 copy-start.3
Sparse Core Ops, SparseCore 0:
  10.5 45.2 all-gather.10
  58.0 40.1 all-gather.12
  100.4 40.1 all-gather.14
  142.6 40.1 all-gather.16
  185.4 40.1 all-gather.18
  237.6 96.8 all-reduce.1
where the time goes:
time: 391 us
  waiting for transfers between devices  272 us (70%)
  matrix products  52.6 us (13%)
  starting transfers between devices  22.9 us (6%)
  other arithmetic  22 us (6%)
  between operations  14.6 us (4%)
  local copies, waits for them, and re-layouts  6.81 us (2%)
    all_gather x5, waiting for transfers between devices, plain_training(): lax.all_gather(hidden_narrow[i], 'tile', axis=0, tiled=True)  166 us
    psum x1, waiting for transfers between devices, plain_training(): upstream = lax.psum(partial_grad, 'tile')  86 us
    dot_general x5, matrix products, plain_training(): jnp.dot(activation, full_hidden[i], preferred_element_type=jnp.float32)  21.8 us
    ppermute x6, waiting for transfers between devices, to_solver(): return lax.ppermute(value.astype(jnp.bfloat16), 'role', [(1, 0)])  11.5 us
    dot_general x5, matrix products, plain_training(): gradient = jnp.dot(own_inputs.T, slope, preferred_element_type=jnp.float32)  10.8 us
    broadcast_in_dim x3, other arithmetic, body(): return (fields_next[None], out_next[None], hidden_next[None])  10.3 us
    ppermute x3, starting transfers between devices, to_trainer(): return lax.ppermute(value.astype(jnp.bfloat16), 'role', [(0, 1)])  10.2 us
    dot_general x3, matrix products, plain_training(): lax.dot_general(slope, full_hidden[i], (((1,), (1,)), ((), ())), preferre...  8.2 us
  transfers between devices with their start and end apart: 17, of which 11 were waited for; matrix products, arithmetic and copies ran while one was open for 18% of the time, Pallas kernels for 0%

commit v1 on v0

--- a/solution.py
+++ b/solution.py
@@ -5,6 +5,10 @@
 
 momentum_decay = 0.9
 step_size = 0.1
+
+
+def read_ladders(array_here, mesh_name):
+    return lax.all_gather(array_here, mesh_name).sum(axis=0)
 
 
 def extended(value, axis, dim, width):
@@ -63,7 +67,7 @@
     partial_grad = lax.dot_general(
         residual, out_narrow, (((1,), (1,)), ((), ())), preferred_element_type=jnp.float32
     )
-    upstream = lax.psum(partial_grad, "tile")
+    upstream = read_ladders(partial_grad, "tile")
     grad_out = jnp.dot(activation.T, residual, preferred_element_type=jnp.float32)
     sent_out = to_solver(grad_out)
     gradients, sent = ([], [])

time: 391 us -> 467 us (1.19)
  waiting for transfers between devices: 272 us -> 338 us
  other arithmetic: 22 us -> 35.8 us
    psum x1 -> x0, waiting for transfers between devices: 86 us -> none  [plain_training(): upstream = lax.psum(partial_grad, 'tile')]
    all_gather x0 -> x1, waiting for transfers between devices: none -> 85.9 us  [read_ladders(): return lax.all_gather(array_here, mesh_name).sum(axis=0)]
    ppermute x3, waiting for transfers between devices: 0.01 us -> 46.9 us  [to_trainer(): return lax.ppermute(value.astype(jnp.bfloat16), 'role', [(0, 1)])]
    all_gather x5, waiting for transfers between devices: 166 us -> 191 us  [plain_training(): lax.all_gather(hidden_narrow[i], 'tile', axis=0, tiled=True)]
    reduce_sum x0 -> x1, other arithmetic: none -> 12.1 us  [read_ladders(): return lax.all_gather(array_here, mesh_name).sum(axis=0)]
    ppermute x1, waiting for transfers between devices: 5.41 us -> 0.01 us  [extended(): before = lax.ppermute(last, axis, up)]
  transfers between devices with their start and end apart: 17 -> 17, of which waited for: 11 -> 12; matrix products, arithmetic and copies ran while one was open for 18% -> 15% of each run, Pallas kernels for 0% -> 0%
where the time goes in v1:
time: 467 us; the launch traced here: 466 us
  waiting for transfers between devices  338 us (72%)
  matrix products  49.1 us (11%)
  other arithmetic  35.8 us (8%)
  starting transfers between devices  20.9 us (4%)
  between operations  14.5 us (3%)
  local copies, waits for them, and re-layouts  7.28 us (2%)
    all_gather x5, waiting for transfers between devices, plain_training(): lax.all_gather(hidden_narrow[i], 'tile', axis=0, tiled=True)  191 us
    all_gather x1, waiting for transfers between devices, read_ladders(): return lax.all_gather(array_here, mesh_name).sum(axis=0)  85.9 us
    ppermute x3, waiting for transfers between devices, to_trainer(): return lax.ppermute(value.astype(jnp.bfloat16), 'role', [(0, 1)])  46.9 us
    dot_general x5, matrix products, plain_training(): jnp.dot(activation, full_hidden[i], preferred_element_type=jnp.float32)  21 us
    reduce_sum x1, other arithmetic, read_ladders(): return lax.all_gather(array_here, mesh_name).sum(axis=0)  12.1 us
    broadcast_in_dim x3, other arithmetic, body(): return (fields_next[None], out_next[None], hidden_next[None])  11.6 us
    dot_general x5, matrix products, plain_training(): gradient = jnp.dot(own_inputs.T, slope, preferred_element_type=jnp.float32)  10.2 us
  transfers between devices with their start and end apart: 17, of which 12 were waited for; matrix products, arithmetic and copies ran while one was open for 15% of the time, Pallas kernels for 0%

profile of v1, /device:TPU:0, one launch (start us, length us, event | category | flops | bytes accessed | tf_op | source)
XLA Modules:
  0.0 465.9 jit_solution(2993543887786085255)
XLA Ops:
  7.2 0.0 all-gather.13.cloned.1.call-start
  7.2 2.4 bitcast_convert_fusion.1
  9.6 2.0 fusion.60
  11.6 0.0 all-gather.15.cloned.1.call-start
  11.7 0.7 all-gather.15.cloned.1.call-update
  12.4 0.7 all-gather.17.cloned.1.call-update
  13.1 0.5 all-gather.19.cloned.1.call-update
  13.7 0.5 all-gather.21.cloned.1.call-update
  14.3 0.0 all-gather.23.cloned.1.call-start
  14.3 3.8 bitcast_convert_fusion
  18.1 37.8 %all-gather.13.cloned.1.call-done = bf16[1,1024,1024]{2,1,0:T(8,128)(2,1)} async-done(((bf16[1,64,1024]{2,1,0:T(8,128)(2,1)}), bf16[1,1024,1024]{2,1,0:T(8,128)(2,1)}) %all-gather.13.cloned.1.call-update) | async-done | bytes 2097168 | tf_op jit(solution)/shard_map/all_gather | solution.py:56
  55.9 4.3 multiply_convert_fusion.10
  60.3 38.0 %all-gather.15.cloned.1.call-done = bf16[1,1024,1024]{2,1,0:T(8,128)(2,1)} async-done(((bf16[1,64,1024]{2,1,0:T(8,128)(2,1)}), bf16[1,1024,1024]{2,1,0:T(8,128)(2,1)}) %all-gather.15.cloned.1.call-update) | async-done | bytes 2097168 | tf_op jit(solution)/shard_map/all_gather | solution.py:56
  98.3 4.4 multiply_convert_fusion.9
  102.7 38.6 %all-gather.17.cloned.1.call-done = bf16[1,1024,1024]{2,1,0:T(8,128)(2,1)} async-done(((bf16[1,64,1024]{2,1,0:T(8,128)(2,1)}), bf16[1,1024,1024]{2,1,0:T(8,128)(2,1)}) %all-gather.17.cloned.1.call-update) | async-done | bytes 2097168 | tf_op jit(solution)/shard_map/all_gather | solution.py:56
  141.3 4.3 multiply_convert_fusion.8
  145.6 38.5 %all-gather.19.cloned.1.call-done = bf16[1,1024,1024]{2,1,0:T(8,128)(2,1)} async-done(((bf16[1,64,1024]{2,1,0:T(8,128)(2,1)}), bf16[1,1024,1024]{2,1,0:T(8,128)(2,1)}) %all-gather.19.cloned.1.call-update) | async-done | bytes 2097168 | tf_op jit(solution)/shard_map/all_gather | solution.py:56
  184.1 4.7 %multiply_convert_fusion.7 = (bf16[512,1024]{1,0:T(8,128)(2,1)}, f32[512,1024]{1,0:T(8,128)}) fusion(bf16[512,1024]{1,0:T(8,128)(2,1)S(1)} %get-tuple-element.18, bf16[1,1024,1024]{2,1,0:T(8,128)(2,1)} %all-gather.19.cloned.1.call-done), kind=kOutput, calls=%fused_computation.45 | convolution fusion | flops 1076363264 | bytes 6291456 | tf_op jit(solution)/shard_map/dot_general | solution.py:62
  188.7 38.1 %all-gather.21.cloned.1.call-done = bf16[1,1024,1024]{2,1,0:T(8,128)(2,1)} async-done(((bf16[1,64,1024]{2,1,0:T(8,128)(2,1)}), bf16[1,1024,1024]{2,1,0:T(8,128)(2,1)}) %all-gather.21.cloned.1.call-update) | async-done | bytes 2097168 | tf_op jit(solution)/shard_map/all_gather | solution.py:56
  226.8 3.3 fusion.10
  230.2 3.7 multiply_convert_fusion.5
  233.9 1.0 copy-done.19
  234.8 4.2 fusion.64
  239.1 0.7 copy-done.10
  239.7 0.1 pad_maximum_fusion.5
  239.9 0.3 collective-permute-start
  240.2 4.9 %collective-permute-start.4 = (bf16[1024,1024]{1,0:T(8,128)(2,1)}, bf16[1024,1024]{1,0:T(8,128)(2,1)}, u32[]{:S(2)}, u32[]{:S(2)}) collective-permute-start(bf16[1024,1024]{1,0:T(8,128)(2,1)} %bitcast_convert_fusion), channel_id=1, source_target_pairs={{0,16},{1,17},{2,18},{3,19},{4,20},{5,21},{6,22},{7,23},{8,24},{9,... | collective-permute-start | bytes 6291464 | tf_op jit(solution)/shard_map/ppermute | solution.py:42
  245.1 3.8 collective-permute-start.1
  248.8 0.1 maximum_reduce_fusion
  249.0 4.1 fusion.61
  253.1 1.5 collective-permute-start.3
  254.5 4.1 collective-permute-done.1
  258.6 0.7 fusion.6
  259.3 2.4 fusion.59
  261.7 1.7 collective-permute-start.2
  263.4 2.1 collective-permute-start.10
  265.6 46.9 %collective-permute-done.2 = bf16[512,1024]{1,0:T(8,128)(2,1)S(1)} collective-permute-done((bf16[512,1024]{1,0:T(8,128)(2,1)}, bf16[512,1024]{1,0:T(8,128)(2,1)S(1)}, u32[]{:S(2)}, u32[]{:S(2)}) %collective-permute-start.2) | collective-permute-done | bytes 1048608 | tf_op jit(solution)/shard_map/ppermute | solution.py:42
  312.5 2.0 gather_fusion
  314.5 3.4 select_bitcast_fusion
  317.9 6.7 %fusion.1 = f32[1,1024,1024]{2,1,0:T(8,128)} fusion(f32[1024,1024]{1,0:T(8,128)} %get-tuple-element.23, f32[1,1024,1024]{2,1,0:T(8,128)S(1)} %copy-done.2, bf16[1024,1024]{1,0:T(8,128)(2,1)} %collective-permute-done.3, bf16[1024,1024]{1,0:T(8,128)(2,1)} %collective-permute-done.4, pred[]{:T(512)S(6)} %eq.4), kind=kLoop, calls=%fused_computation.4 | loop fusion | flops 9437184 | bytes 16777216 | tf_op jit(solution)/shard_map/broadcast_in_dim | solution.py:121
  324.6 85.9 %all-gather.23.cloned.1.call-done = f32[8192,1024]{1,0:T(8,128)} async-done(((f32[512,1024]{1,0:T(8,128)}), f32[8192,1024]{1,0:T(8,128)}) %all-gather.23.cloned.1.call-update) | async-done | bytes 33554448 | tf_op jit(solution)/shard_map/all_gather | solution.py:11
  410.5 12.1 %reduce_sum.9 = f32[512,1024]{1,0:T(8,128)S(1)} reduce(f32[16,512,1024]{2,1,0:T(8,128)} %bitcast.104, f32[]{:T(128)} %constant.19.clone.1), dimensions={0}, to_apply=%region_0.1 | reduce | flops 7864320 | bytes 35651588 | tf_op jit(solution)/shard_map/reduce_sum | solution.py:11
  422.6 2.5 multiply_convert_fusion.4
  425.1 0.3 copy-done.23
  425.4 1.6 multiply_convert_fusion.3
  427.1 0.6 copy-done.22
  427.7 1.6 multiply_convert_fusion.2
  429.3 0.6 copy-done.21
  429.9 2.6 multiply_convert_fusion.1
  432.5 4.3 bitcast_dynamic-update-slice_fusion.4
  436.8 1.8 bitcast_dynamic-update-slice_fusion.3
  438.7 1.3 collective-permute-start.6
  440.0 1.3 collective-permute-start.5
  441.3 1.3 bitcast_dynamic-update-slice_fusion.2
  442.6 1.3 collective-permute-start.7
  443.9 1.4 bitcast_dynamic-update-slice_fusion.1
  445.3 1.3 collective-permute-start.8
  446.7 1.3 bitcast_dynamic-update-slice_fusion
  448.0 1.8 collective-permute-done.5
  449.8 1.3 collective-permute-start.9
  451.1 1.5 collective-permute-done.7
  452.6 2.8 collective-permute-done.8
  455.4 2.1 collective-permute-done.9
  457.5 1.6 fusion.35
  (61 shorter events, 0.3 us)
Async XLA Ops:
  7.2 48.8 %copy-start = (bf16[512,1024]{1,0:T(8,128)(2,1)S(1)}, bf16[512,1024]{1,0:T(8,128)(2,1)}, u32[]{:S(2)}) copy-start(bf16[512,1024]{1,0:T(8,128)(2,1)} %param.10) | copy-start | bytes 3145732
  7.2 48.8 %all-gather.13.cloned.1.call-start = ((), (), s32[]{:S(2)}) async-start(), calls=%async_computation | async-start | bytes 2228224 | tf_op jit(solution)/shard_map/all_gather | solution.py:56
  11.6 86.7 %all-gather.15.cloned.1.call-start = ((), (), s32[]{:S(2)}) async-start(), calls=%async_computation.1 | async-start | bytes 2228224 | tf_op jit(solution)/shard_map/all_gather | solution.py:56
  12.4 128.9 %all-gather.17.cloned.1.call-start = ((), (), s32[]{:S(2)}) async-start(), calls=%async_computation.2 | async-start | bytes 2228224 | tf_op jit(solution)/shard_map/all_gather | solution.py:56
  13.1 171.0 %all-gather.19.cloned.1.call-start = ((), (), s32[]{:S(2)}) async-start(), calls=%async_computation.3 | async-start | bytes 2228224 | tf_op jit(solution)/shard_map/all_gather | solution.py:56
  13.7 213.2 %all-gather.21.cloned.1.call-start = ((), (), s32[]{:S(2)}) async-start(), calls=%async_computation.4 | async-start | bytes 2228224 | tf_op jit(solution)/shard_map/all_gather | solution.py:56
  14.3 396.2 %all-gather.23.cloned.1.call-start = ((), (), s32[]{:S(2)}) async-start(), calls=%async_computation.5 | async-start | bytes 35651584 | tf_op jit(solution)/shard_map/all_gather | solution.py:11
  60.3 42.4 %copy-start.13 = (bf16[512,1024]{1,0:T(8,128)(2,1)}, bf16[512,1024]{1,0:T(8,128)(2,1)S(1)}, u32[]{:S(2)}) copy-start(bf16[512,1024]{1,0:T(8,128)(2,1)S(1)} %get-tuple-element.14) | copy-start | bytes 3145732
  102.7 42.9 %copy-start.12 = (bf16[512,1024]{1,0:T(8,128)(2,1)}, bf16[512,1024]{1,0:T(8,128)(2,1)S(1)}, u32[]{:S(2)}) copy-start(bf16[512,1024]{1,0:T(8,128)(2,1)S(1)} %get-tuple-element.16) | copy-start | bytes 3145732
  145.6 43.2 %copy-start.11 = (bf16[512,1024]{1,0:T(8,128)(2,1)}, bf16[512,1024]{1,0:T(8,128)(2,1)S(1)}, u32[]{:S(2)}) copy-start(bf16[512,1024]{1,0:T(8,128)(2,1)S(1)} %get-tuple-element.18) | copy-start | bytes 3145732
  226.8 3.3 copy-start.1
  230.2 3.7 copy-start.6
  233.8 1.0 copy-start.19
  239.0 0.7 copy-start.10
  239.7 9.2 %copy-start.7 = (f32[512,1024]{1,0:T(8,128)S(1)}, f32[512,1024]{1,0:T(8,128)}, u32[]{:S(2)}) copy-start(f32[512,1024]{1,0:T(8,128)} %copy-done.6) | copy-start | bytes 6291460
  239.7 9.2 %copy-start.20 = (bf16[512,1024]{1,0:T(8,128)(2,1)S(1)}, bf16[512,1024]{1,0:T(8,128)(2,1)}, u32[]{:S(2)}) copy-start(bf16[512,1024]{1,0:T(8,128)(2,1)} %copy-done.19) | copy-start | bytes 3145732
  239.9 9.0 %collective-permute-start = (f32[513,1]{1,0:T(8,128)S(1)}, f32[513,1]{1,0:T(8,128)S(1)}, u32[]{:S(2)}, u32[]{:S(2)}) collective-permute-start(f32[513,1]{1,0:T(8,128)S(1)} %get-tuple-element.7), channel_id=1, source_target_pairs={{0,1},{1,2},{2,3},{3,4},{4,5},{5,6},{6,7},{7,8},{8,9},{9,10},{10,1... | collective-permute-start | bytes 6164 | tf_op jit(solution)/shard_map/ppermute | solution.py:20
  240.2 77.8 %collective-permute-start.4 = (bf16[1024,1024]{1,0:T(8,128)(2,1)}, bf16[1024,1024]{1,0:T(8,128)(2,1)}, u32[]{:S(2)}, u32[]{:S(2)}) collective-permute-start(bf16[1024,1024]{1,0:T(8,128)(2,1)} %bitcast_convert_fusion), channel_id=1, source_target_pairs={{0,16},{1,17},{2,18},{3,19},{4,20},{5,21},{6,22},{7,23},{8,24},{9,... | collective-permute-start | bytes 6291464 | tf_op jit(solution)/shard_map/ppermute | solution.py:42
  245.1 13.5 %collective-permute-start.1 = (f32[513,1]{1,0:T(8,128)S(1)}, f32[513,1]{1,0:T(8,128)S(1)}, u32[]{:S(2)}, u32[]{:S(2)}) collective-permute-start(f32[513,1]{1,0:T(8,128)S(1)} %get-tuple-element.8), channel_id=1, source_target_pairs={{1,0},{2,1},{3,2},{4,3},{5,4},{6,5},{7,6},{8,7},{9,8},{10,9},{11,1... | collective-permute-start | bytes 6164 | tf_op jit(solution)/shard_map/ppermute | solution.py:21
  253.1 64.9 %collective-permute-start.3 = (bf16[1024,1024]{1,0:T(8,128)(2,1)}, bf16[1024,1024]{1,0:T(8,128)(2,1)}, u32[]{:S(2)}, u32[]{:S(2)}) collective-permute-start(bf16[1024,1024]{1,0:T(8,128)(2,1)} %get-tuple-element.22), channel_id=1, source_target_pairs={{16,0},{17,1},{18,2},{19,3},{20,4},{21,5},{22,6},{23,7},{24,8},{25... | collective-permute-start | bytes 6291464 | tf_op jit(solution)/shard_map/ppermute | solution.py:46
  258.6 0.7 copy-start.15
  259.3 6.3 %copy-start.14 = (s32[512]{0:T(512)S(1)}, s32[512]{0:T(512)}, u32[]{:S(2)}) copy-start(s32[512]{0:T(512)} %param.11) | copy-start | bytes 6148
  261.7 50.7 %collective-permute-start.2 = (bf16[512,1024]{1,0:T(8,128)(2,1)}, bf16[512,1024]{1,0:T(8,128)(2,1)S(1)}, u32[]{:S(2)}, u32[]{:S(2)}) collective-permute-start(bf16[512,1024]{1,0:T(8,128)(2,1)} %get-tuple-element.5), channel_id=1, source_target_pairs={{0,16},{1,17},{2,18},{3,19},{4,20},{5,21},{6,22},{7,23},{8,24},{9,... | collective-permute-start | bytes 3145736 | tf_op jit(solution)/shard_map/ppermute | solution.py:42
  263.4 194.0 %collective-permute-start.10 = (bf16[5,64,1024]{2,1,0:T(8,128)(2,1)}, bf16[5,64,1024]{2,1,0:T(8,128)(2,1)}, u32[]{:S(2)}, u32[]{:S(2)}) collective-permute-start(bf16[5,64,1024]{2,1,0:T(8,128)(2,1)} %bitcast_convert_fusion.1), channel_id=1, source_target_pairs={{0,16},{1,17},{2,18},{3,19},{4,20},{5,21},{6,22},{7,23},{8,24},{9,... | collective-permute-start | bytes 1966088 | tf_op jit(solution)/shard_map/ppermute | solution.py:42
  314.5 3.4 copy-start.2
  422.6 2.5 copy-start.18
  422.6 2.8 copy-start.23
  425.1 2.0 copy-start.4
  425.4 1.7 copy-start.17
  425.4 2.2 copy-start.22
  427.7 1.7 copy-start.16
  427.7 2.2 copy-start.21
  429.3 3.2 copy-start.8
  436.8 4.5 copy-start.9
  436.8 9.8 %copy-start.5 = (bf16[512,1024]{1,0:T(8,128)(2,1)S(1)}, bf16[512,1024]{1,0:T(8,128)(2,1)}, u32[]{:S(2)}) copy-start(bf16[512,1024]{1,0:T(8,128)(2,1)} %copy-done.4) | copy-start | bytes 3145732
  438.7 12.4 %collective-permute-start.6 = (bf16[64,1024]{1,0:T(8,128)(2,1)S(1)}, bf16[64,1024]{1,0:T(8,128)(2,1)S(1)}, u32[]{:S(2)}, u32[]{:S(2)}) collective-permute-start(bf16[64,1024]{1,0:T(8,128)(2,1)S(1)} %get-tuple-element.27), channel_id=1, source_target_pairs={{16,0},{17,1},{18,2},{19,3},{20,4},{21,5},{22,6},{23,7},{24,8},{25... | collective-permute-start | bytes 393224 | tf_op jit(solution)/shard_map/ppermute | solution.py:46
  440.0 9.8 %collective-permute-start.5 = (bf16[64,1024]{1,0:T(8,128)(2,1)S(1)}, bf16[64,1024]{1,0:T(8,128)(2,1)S(1)}, u32[]{:S(2)}, u32[]{:S(2)}) collective-permute-start(bf16[64,1024]{1,0:T(8,128)(2,1)S(1)} %get-tuple-element.25), channel_id=1, source_target_pairs={{16,0},{17,1},{18,2},{19,3},{20,4},{21,5},{22,6},{23,7},{24,8},{25... | collective-permute-start | bytes 393224 | tf_op jit(solution)/shard_map/ppermute | solution.py:46
  442.6 10.0 %collective-permute-start.7 = (bf16[64,1024]{1,0:T(8,128)(2,1)S(1)}, bf16[64,1024]{1,0:T(8,128)(2,1)S(1)}, u32[]{:S(2)}, u32[]{:S(2)}) collective-permute-start(bf16[64,1024]{1,0:T(8,128)(2,1)S(1)} %get-tuple-element.29), channel_id=1, source_target_pairs={{16,0},{17,1},{18,2},{19,3},{20,4},{21,5},{22,6},{23,7},{24,8},{25... | collective-permute-start | bytes 393224 | tf_op jit(solution)/shard_map/ppermute | solution.py:46
  443.9 13.6 %copy-start.3 = (f32[1,5,64,1024]{3,2,1,0:T(8,128)S(1)}, f32[1,5,64,1024]{3,2,1,0:T(8,128)}, u32[]{:S(2)}) copy-start(f32[1,5,64,1024]{3,2,1,0:T(8,128)} %param.13) | copy-start | bytes 3932164
  445.3 10.0 %collective-permute-start.8 = (bf16[64,1024]{1,0:T(8,128)(2,1)S(1)}, bf16[64,1024]{1,0:T(8,128)(2,1)S(1)}, u32[]{:S(2)}, u32[]{:S(2)}) collective-permute-start(bf16[64,1024]{1,0:T(8,128)(2,1)S(1)} %get-tuple-element.31), channel_id=1, source_target_pairs={{16,0},{17,1},{18,2},{19,3},{20,4},{21,5},{22,6},{23,7},{24,8},{25... | collective-permute-start | bytes 393224 | tf_op jit(solution)/shard_map/ppermute | solution.py:46
  449.8 7.7 %collective-permute-start.9 = (bf16[64,1024]{1,0:T(8,128)(2,1)S(1)}, bf16[64,1024]{1,0:T(8,128)(2,1)S(1)}, u32[]{:S(2)}, u32[]{:S(2)}) collective-permute-start(bf16[64,1024]{1,0:T(8,128)(2,1)S(1)} %get-tuple-element.33), channel_id=1, source_target_pairs={{16,0},{17,1},{18,2},{19,3},{20,4},{21,5},{22,6},{23,7},{24,8},{25... | collective-permute-start | bytes 393224 | tf_op jit(solution)/shard_map/ppermute | solution.py:46
Sparse Core Ops, SparseCore 0:
  11.7 44.1 all-gather.12
  58.1 40.1 all-gather.14
  101.0 40.1 all-gather.16
  143.8 40.1 all-gather.18
  186.6 40.1 all-gather.20
  239.2 171.2 all-gather.22
